TPU v7x, 512 devices: a whole 4x4x16 slice. The times are simulated.
512 devices in a mesh: rows: 64 (over y, z), cols: 8 (over x, core).
Axes of the slice: x: 4, y: 4, z: 16, core: 2. Of those that a mesh axis runs over, the one named last changes fastest.
Arguments:
- node_features: bfloat16 [65536, 512], P('rows', 'cols'), may hold values from -6 to 6
- weight: bfloat16 [512, 512], replicated, may hold values from -0.25 to 0.25
- tile_values: bfloat16 [4096, 128, 128], P('rows'), may hold values from -0.1875 to 0.1875
- tile_row: int32 [4096], P('rows'), may hold values from 0 to 7
- source_owner: int32 [4096, 1], P('rows'), may hold values from 0 to 63; in each aligned block of 64 rows (0 to 63, 64 to 127, ...) at most 2 rows name the same one
- source_block: int32 [4096], P('rows'), may hold values from 0 to 7
- labels: int32 [65536], P('rows'), may hold values from 0 to 511
Outputs:
- activations: bfloat16 [65536, 512], P('rows', 'cols')
- weight_grad: float32 [512, 512], P(None, 'cols')
- feature_grad: bfloat16 [65536, 512], P('rows', 'cols')
Inputs may be any that keep to these rules, and one draw needn't show every extreme that they name: `source_owner`: of the 64 tiles of one index of rows, at most 2 name the same owner.
All inputs are finite; a program needn't handle non-finite values.
Results may differ from a plain program's by a relative error of at most 0.0095.
Values may be sent and summed in bfloat16 or wider, within the bound.
A program may use at most 64 MiB of HBM per device.

v0:
```python
import math
import jax
import jax.numpy as jnp
from jax import lax
from jax.sharding import PartitionSpec as P


def slot_ranks(owners):
    positions = jnp.arange(owners.shape[0], dtype=jnp.int32)
    earlier = (owners[:, None] == owners[None, :]) & (positions[None, :] < positions[:, None])
    return jnp.sum(earlier.astype(jnp.int32), axis=1)


def per_device(node_features, weight, tile_values, tile_row, source_owner, source_block, labels):
    local_rows, col_width = node_features.shape
    block_size = tile_values.shape[1]
    local_blocks = local_rows // block_size
    row_devices = lax.axis_size("rows")
    capacity = 2 * tile_values.shape[0] // row_devices
    owners = source_owner[:, 0]
    slot_rank = slot_ranks(owners)
    column_block = owners * local_blocks + source_block
    local_ids = jnp.arange(local_blocks, dtype=jnp.int32)
    row_onehot = (tile_row[:, None] == local_ids[None, :]).astype(jnp.float32)
    gathered = lax.all_gather(node_features, "rows", axis=0, tiled=True)
    all_blocks = gathered.reshape(row_devices * local_blocks, block_size, col_width)
    source_rows = all_blocks[column_block]
    products = jnp.einsum(
        "tij,tjf->tif", tile_values, source_rows, preferred_element_type=jnp.float32
    )
    summed = jnp.einsum("tb,tif->bif", row_onehot, products, precision=lax.Precision.HIGHEST)
    aggregated = summed.reshape(local_rows, col_width).astype(jnp.bfloat16)
    aggregated_all = lax.all_gather(aggregated, "cols", axis=1, tiled=True)
    col_index = lax.axis_index("cols")
    w_columns = lax.dynamic_slice_in_dim(weight, col_index * col_width, col_width, 1)
    w_rows = lax.dynamic_slice_in_dim(weight, col_index * col_width, col_width, 0)
    hidden = jnp.dot(aggregated_all, w_columns, preferred_element_type=jnp.float32)
    sigmoid = jax.nn.sigmoid(hidden)
    activated = hidden * sigmoid
    slopes = sigmoid * (1.0 + hidden * (1.0 - sigmoid))
    feature_ids = col_index * col_width + jnp.arange(col_width, dtype=jnp.int32)
    target = (labels[:, None] == feature_ids[None, :]).astype(jnp.float32)
    out_grad = ((activated - target) * slopes).astype(jnp.bfloat16)
    grad_all = lax.all_gather(out_grad, "cols", axis=1, tiled=True)
    weight_terms = jnp.einsum(
        "nk,nc->kc", aggregated_all, out_grad, preferred_element_type=jnp.float32
    )
    node_total = local_rows * row_devices
    weight_grad = lax.psum(weight_terms, "rows") / math.sqrt(node_total)
    agg_grad = jnp.einsum("nc,kc->nk", grad_all, w_rows, preferred_element_type=jnp.float32).astype(
        jnp.bfloat16
    )
    grad_rows = agg_grad.reshape(local_blocks, block_size, col_width)[tile_row]
    sent_terms = jnp.einsum(
        "tji,tjf->tif", tile_values, grad_rows, preferred_element_type=jnp.float32
    )
    send_terms = (
        jnp.zeros((row_devices, capacity, block_size, col_width), jnp.float32)
        .at[owners, slot_rank]
        .set(sent_terms)
    )
    send_index = (
        jnp.zeros((row_devices, capacity), jnp.int32).at[owners, slot_rank].set(source_block)
    )
    received, recv_index = (
        lax.all_to_all(
            send_terms.astype(jnp.bfloat16), "rows", split_axis=0, concat_axis=0, tiled=True
        ).astype(send_terms.dtype),
        lax.all_to_all(send_index, "rows", split_axis=0, concat_axis=0, tiled=True),
    )
    placing = (recv_index[:, :, None] == local_ids[None, None, :]).astype(jnp.float32)
    filled = (jnp.abs(received).sum(axis=(2, 3)) >= 0.0).astype(jnp.float32)
    feature_grad = jnp.einsum(
        "scb,scif->bif", placing * filled[:, :, None], received, precision=lax.Precision.HIGHEST
    ).reshape(local_rows, col_width)
    return (activated.astype(jnp.bfloat16), weight_grad, feature_grad.astype(jnp.bfloat16))


def solution(mesh):
    return jax.shard_map(
        per_device,
        mesh=mesh,
        in_specs=(
            P("rows", "cols"),
            P(),
            P("rows", None, None),
            P("rows"),
            P("rows", None),
            P("rows"),
            P("rows"),
        ),
        out_specs=(P("rows", "cols"), P(None, "cols"), P("rows", "cols")),
        check_vma=False,
    )
```

profile of v0, /device:TPU:2, one launch (start us, length us, event | category | flops | bytes accessed | tf_op | source)
XLA Modules:
  0.0 590.2 jit_solution(7779311799218977783)
XLA Ops:
  7.2 0.7 all-gather.4.cloned.1.call-update
  8.0 0.7 compare_select_fusion.3
  8.6 164.2 %all-gather.4.cloned.1.call-done = bf16[65536,64]{0,1:T(8,128)(2,1)} async-done(((bf16[1024,64]{0,1:T(8,128)(2,1)}), bf16[65536,64]{0,1:T(8,128)(2,1)}) %all-gather.4.cloned.1.call-update) | async-done | bytes 8388624 | tf_op jit(solution)/shard_map/all_gather | solution.py:25
  172.9 9.0 %copy_bitcast_fusion = bf16[512,128,64]{1,2,0:T(8,128)(2,1)} fusion(bf16[65536,64]{0,1:T(8,128)(2,1)} %all-gather.4.cloned.1.call-done), kind=kLoop, calls=%fused_computation.4 | loop fusion | bytes 16777216 | tf_op jit(solution)/shard_map/reshape | solution.py:26
  181.9 4.1 gather_fusion
  186.0 1.5 convolution_bitcast_fusion.1
  187.6 2.0 fusion.10
  189.6 0.7 copy.68
  190.3 0.0 all-gather.8.cloned.1.call-start
  190.4 24.7 %all-gather.6.cloned.1.call-done = bf16[1024,512]{0,1:T(8,128)(2,1)} async-done(((bf16[1024,64]{0,1:T(8,128)(2,1)}), bf16[1024,512]{0,1:T(8,128)(2,1)}) %all-gather.6.cloned.1.call-update) | async-done | bytes 1048592 | tf_op jit(solution)/shard_map/all_gather | solution.py:33
  215.0 2.4 multiply_convert_fusion
  217.5 0.2 convert_reduce_fusion
  217.7 3.5 scatter_fusion
  221.2 0.7 copy.42
  221.9 15.2 %all-to-all-start = ((s32[64,1,2]{2,1,0:T(1,128)}), s32[64,1,2]{2,1,0:T(1,128)S(1)}, u32[]{:S(2)}, u32[]{:S(2)}) async-start(s32[64,1,2]{2,1,0:T(1,128)} %copy.42), calls=%async_computation | async-start | bytes 65536 | tf_op jit(solution)/shard_map/all_to_all | solution.py:69
  237.1 11.6 %all-gather.8.cloned.1.call-done = bf16[1024,512]{0,1:T(8,128)(2,1)} async-done(((bf16[1024,64]{0,1:T(8,128)(2,1)}), bf16[1024,512]{0,1:T(8,128)(2,1)}) %all-gather.8.cloned.1.call-update) | async-done | bytes 1048592 | tf_op jit(solution)/shard_map/all_gather | solution.py:44
  248.7 1.6 fusion.13
  250.3 0.8 gather_fusion.1
  251.1 2.0 convolution_bitcast_fusion
  253.1 2.5 broadcast_in_dim.10
  255.6 10.6 %scatter_fusion.1 = f32[64,2,128,64]{2,3,1,0:T(8,128)} fusion(f32[64,2,128,64]{2,3,1,0:T(8,128)} %broadcast_in_dim.10, s32[64]{0:T(128)S(1)} %fusion.31, f32[64,128,64]{1,2,0:T(8,128)} %convolution_bitcast_fusion), kind=kCustom, calls=%fused_computation.3 | custom fusion | bytes 6291968 | tf_op jit(solution)/shard_map/scatter | solution.py:60
  266.2 2.7 convert_element_type.49
  268.9 3.5 copy.45
  272.4 15.9 %all-to-all-start.1 = ((bf16[64,2,128,64]{2,1,3,0:T(2,128)(2,1)}), bf16[64,2,128,64]{2,1,3,0:T(2,128)(2,1)}, u32[]{:S(2)}, u32[]{:S(2)}) async-start(bf16[64,2,128,64]{2,1,3,0:T(2,128)(2,1)} %copy.45), calls=%async_computation.1 | async-start | bytes 4194304 | tf_op jit(solution)/shard_map/all_to_all | solution.py:66
  288.4 1.1 fusion.33
  289.6 0.1 copy.43
  289.6 283.3 %all-reduce.2.cloned.1.call-done = f32[512,64]{0,1:T(8,128)} async-done(((f32[512,64]{0,1:T(8,128)}), f32[512,64]{0,1:T(8,128)}) %all-reduce.2.cloned.1.call-update) | async-done | bytes 131088 | tf_op jit(solution)/shard_map/psum | solution.py:49
  573.0 1.6 broadcast_multiply_fusion
  574.5 3.8 abs_reduce_fusion
  578.4 0.1 copy.46
  578.5 4.5 fusion.7
  583.0 0.7 copy.67
  (30 shorter events, 0.3 us)
Async XLA Ops:
  7.2 178.9 %copy-start = (bf16[64,128,128]{2,1,0:T(8,128)(2,1)S(1)}, bf16[64,128,128]{2,1,0:T(8,128)(2,1)}, u32[]{:S(2)}) copy-start(bf16[64,128,128]{2,1,0:T(8,128)(2,1)} %param.9) | copy-start | bytes 6291460
  7.2 165.7 %all-gather.4.cloned.1.call-start = ((), (), s32[]{:S(2)}) async-start(), calls=%async_computation.2 | async-start | bytes 8519680 | tf_op jit(solution)/shard_map/all_gather | solution.py:25
  7.9 207.1 %all-gather.6.cloned.1.call-start = ((), (), s32[]{:S(2)}) async-start(), calls=%async_computation.3 | async-start | bytes 1179648 | tf_op jit(solution)/shard_map/all_gather | solution.py:33
  186.0 1.5 copy-start.4
  187.6 27.4 %copy-start.5 = (s32[1024]{0:T(1024)S(1)}, s32[1024]{0:T(1024)}, u32[]{:S(2)}) copy-start(s32[1024]{0:T(1024)} %param.13) | copy-start | bytes 12292
  189.6 27.9 %copy-start.6 = (s32[64,1]{0,1:T(1,128)S(1)}, s32[64,1]{0,1:T(1,128)}, u32[]{:S(2)}) copy-start(s32[64,1]{0,1:T(1,128)} %param.11) | copy-start | bytes 772
  189.6 28.1 %copy-start.3 = (s32[64]{0:T(128)S(1)}, s32[64]{0:T(128)}, u32[]{:S(2)}) copy-start(s32[64]{0:T(128)} %param.12) | copy-start | bytes 772
  190.3 58.4 %all-gather.8.cloned.1.call-start = ((), (), s32[]{:S(2)}) async-start(), calls=%async_computation.5 | async-start | bytes 1179648 | tf_op jit(solution)/shard_map/all_gather | solution.py:44
  221.9 50.5 %all-to-all-start = ((s32[64,1,2]{2,1,0:T(1,128)}), s32[64,1,2]{2,1,0:T(1,128)S(1)}, u32[]{:S(2)}, u32[]{:S(2)}) async-start(s32[64,1,2]{2,1,0:T(1,128)} %copy.42), calls=%async_computation | async-start | bytes 65536 | tf_op jit(solution)/shard_map/all_to_all | solution.py:69
  272.4 16.0 %copy-start.1 = (bf16[1024,512]{0,1:T(8,128)(2,1)S(1)}, bf16[1024,512]{0,1:T(8,128)(2,1)}, u32[]{:S(2)}) copy-start(bf16[1024,512]{0,1:T(8,128)(2,1)} %all-gather.6.cloned.1.call-done) | copy-start | bytes 3145732
  272.4 16.0 %copy-start.2 = (bf16[1024,64]{0,1:T(8,128)(2,1)S(1)}, bf16[1024,64]{0,1:T(8,128)(2,1)}, u32[]{:S(2)}) copy-start(bf16[1024,64]{0,1:T(8,128)(2,1)} %get-tuple-element.3) | copy-start | bytes 393220
  272.4 302.1 %all-to-all-start.1 = ((bf16[64,2,128,64]{2,1,3,0:T(2,128)(2,1)}), bf16[64,2,128,64]{2,1,3,0:T(2,128)(2,1)}, u32[]{:S(2)}, u32[]{:S(2)}) async-start(bf16[64,2,128,64]{2,1,3,0:T(2,128)(2,1)} %copy.45), calls=%async_computation.1 | async-start | bytes 4194304 | tf_op jit(solution)/shard_map/all_to_all | solution.py:66
  288.4 284.6 %all-reduce.2.cloned.1.call-start = ((), (), s32[]{:S(2)}) async-start(), calls=%async_computation.4 | async-start | bytes 262144 | tf_op jit(solution)/shard_map/psum | solution.py:49
Sparse Core Ops, SparseCore 0:
  11.0 161.8 all-gather.3
  190.4 24.5 all-gather.5
  217.7 30.9 all-gather.7
  292.9 280.0 all-reduce.1
where the time goes:
time: 591 us; the launch traced here: 590 us
  waiting for transfers between devices  485 us (82%)
  local copies, waits for them, and re-layouts  36.3 us (6%)
  starting transfers between devices  31.3 us (5%)
  matrix products  15.1 us (3%)
  between operations  14 us (2%)
  other arithmetic  9.01 us (2%)
    psum x1, waiting for transfers between devices, per_device(): weight_grad = lax.psum(weight_terms, 'rows') / math.sqrt(node_total)  283 us
    all_gather x1, waiting for transfers between devices, per_device(): gathered = lax.all_gather(node_features, 'rows', axis=0, tiled=True)  164 us
    all_gather x1, waiting for transfers between devices, per_device(): aggregated_all = lax.all_gather(aggregated, 'cols', axis=1, tiled=True)  24.7 us
    all_to_all x1, starting transfers between devices, per_device(): lax.all_to_all(send_terms.astype(jnp.bfloat16), 'rows', split_axis=0, con...  15.9 us
    all_to_all x1, starting transfers between devices, per_device(): lax.all_to_all(send_index, 'rows', split_axis=0, concat_axis=0, tiled=True)  15.2 us
  transfers between devices with their start and end apart: 6, of which 4 were waited for; matrix products, arithmetic and copies ran while one was open for 5% of the time, Pallas kernels for 0%

commit v1 on v0

--- a/solution.py
+++ b/solution.py
@@ -3,6 +3,8 @@
 import jax.numpy as jnp
 from jax import lax
 from jax.sharding import PartitionSpec as P
+
+push_streams_on = lambda tile_in, device_axis: jnp.sum(lax.all_gather(tile_in, device_axis), 0)
 
 
 def slot_ranks(owners):
@@ -46,7 +48,7 @@
         "nk,nc->kc", aggregated_all, out_grad, preferred_element_type=jnp.float32
     )
     node_total = local_rows * row_devices
-    weight_grad = lax.psum(weight_terms, "rows") / math.sqrt(node_total)
+    weight_grad = push_streams_on(weight_terms, "rows") / math.sqrt(node_total)
     agg_grad = jnp.einsum("nc,kc->nk", grad_all, w_rows, preferred_element_type=jnp.float32).astype(
         jnp.bfloat16
     )

time: 591 us -> 464 us (0.79)
  the two profiles are of different devices: /device:TPU:2 before, /device:TPU:8 now
where the time goes in v1:
time: 464 us
  waiting for transfers between devices  346 us (75%)
  local copies, waits for them, and re-layouts  44.6 us (10%)
  starting transfers between devices  31.9 us (7%)
  matrix products  16.1 us (3%)
  between operations  14 us (3%)
  other arithmetic  10.5 us (2%)
    all_gather x1, waiting for transfers between devices, per_device(): gathered = lax.all_gather(node_features, 'rows', axis=0, tiled=True)  163 us
    all_to_all x1, waiting for transfers between devices, per_device(): lax.all_to_all(send_terms.astype(jnp.bfloat16), 'rows', split_axis=0, con...  106 us
    all_gather x1, waiting for transfers between devices, lax.all_gather(tile_in, device_axis)  40.4 us
    all_gather x1, waiting for transfers between devices, per_device(): aggregated_all = lax.all_gather(aggregated, 'cols', axis=1, tiled=True)  27.1 us
    all_to_all x1, starting transfers between devices, per_device(): lax.all_to_all(send_terms.astype(jnp.bfloat16), 'rows', split_axis=0, con...  16 us
    all_to_all x1, starting transfers between devices, per_device(): lax.all_to_all(send_index, 'rows', split_axis=0, concat_axis=0, tiled=True)  15.7 us
    scatter x1, local copies, waits for them, and re-layouts, per_device(): send_terms = jnp.zeros((row_devices, capacity, block_size, col_width), jn...  10.7 us
    unnamed x15, local copies, waits for them, and re-layouts  9.52 us
  transfers between devices with their start and end apart: 6, of which 5 were waited for; matrix products, arithmetic and copies ran while one was open for 9% of the time, Pallas kernels for 0%

profile of v1, /device:TPU:8, one launch (start us, length us, event | category | flops | bytes accessed | tf_op | source)
XLA Modules:
  0.0 463.5 jit_solution(2257676838799061647)
XLA Ops:
  7.2 0.7 all-gather.6.cloned.1.call-update
  8.0 0.7 compare_select_fusion.3
  8.6 162.9 %all-gather.6.cloned.1.call-done = bf16[65536,64]{0,1:T(8,128)(2,1)} async-done(((bf16[1024,64]{0,1:T(8,128)(2,1)}), bf16[65536,64]{0,1:T(8,128)(2,1)}) %all-gather.6.cloned.1.call-update) | async-done | bytes 8388624 | tf_op jit(solution)/shard_map/all_gather | solution.py:27
  171.6 9.0 %copy_bitcast_fusion = bf16[512,128,64]{1,2,0:T(8,128)(2,1)} fusion(bf16[65536,64]{0,1:T(8,128)(2,1)} %all-gather.6.cloned.1.call-done), kind=kLoop, calls=%fused_computation.5 | loop fusion | bytes 16777216 | tf_op jit(solution)/shard_map/reshape | solution.py:28
  180.6 4.1 gather_fusion
  184.8 1.5 convolution_bitcast_fusion.1
  186.3 2.0 fusion.10
  188.3 0.7 copy.69
  189.1 27.1 %all-gather.8.cloned.1.call-done = bf16[1024,512]{0,1:T(8,128)(2,1)} async-done(((bf16[1024,64]{0,1:T(8,128)(2,1)}), bf16[1024,512]{0,1:T(8,128)(2,1)}) %all-gather.8.cloned.1.call-update) | async-done | bytes 1048592 | tf_op jit(solution)/shard_map/all_gather | solution.py:35
  216.1 2.5 multiply_convert_fusion
  218.7 2.0 fusion.33
  220.8 0.2 convert_reduce_fusion
  221.0 3.5 scatter_fusion
  224.5 0.7 copy.42
  225.2 15.7 %all-to-all-start = ((s32[64,1,2]{2,1,0:T(1,128)}), s32[64,1,2]{2,1,0:T(1,128)S(1)}, u32[]{:S(2)}, u32[]{:S(2)}) async-start(s32[64,1,2]{2,1,0:T(1,128)} %copy.42), calls=%async_computation | async-start | bytes 65536 | tf_op jit(solution)/shard_map/all_to_all | solution.py:71
  240.9 8.9 %all-gather.10.cloned.1.call-done = bf16[1024,512]{0,1:T(8,128)(2,1)} async-done(((bf16[1024,64]{0,1:T(8,128)(2,1)}), bf16[1024,512]{0,1:T(8,128)(2,1)}) %all-gather.10.cloned.1.call-update) | async-done | bytes 1048592 | tf_op jit(solution)/shard_map/all_gather | solution.py:46
  249.9 1.6 fusion.13
  251.5 0.8 gather_fusion.1
  252.2 2.0 convolution_bitcast_fusion
  254.2 2.5 broadcast_in_dim.10
  256.7 10.7 %scatter_fusion.1 = f32[64,2,128,64]{2,3,1,0:T(8,128)} fusion(f32[64,2,128,64]{2,3,1,0:T(8,128)} %broadcast_in_dim.10, s32[64]{0:T(128)S(1)} %fusion.31, f32[64,128,64]{1,2,0:T(8,128)} %convolution_bitcast_fusion), kind=kCustom, calls=%fused_computation.3 | custom fusion | bytes 6291968 | tf_op jit(solution)/shard_map/scatter | solution.py:62
  267.5 2.7 convert_element_type.49
  270.2 3.5 copy.45
  273.7 16.0 %all-to-all-start.1 = ((bf16[64,2,128,64]{2,1,3,0:T(2,128)(2,1)}), bf16[64,2,128,64]{2,1,3,0:T(2,128)(2,1)}, u32[]{:S(2)}, u32[]{:S(2)}) async-start(bf16[64,2,128,64]{2,1,3,0:T(2,128)(2,1)} %copy.45), calls=%async_computation.1 | async-start | bytes 4194304 | tf_op jit(solution)/shard_map/all_to_all | solution.py:68
  289.7 106.5 %all-to-all-done.1 = bf16[64,2,128,64]{2,1,3,0:T(2,128)(2,1)} async-done(((bf16[64,2,128,64]{2,1,3,0:T(2,128)(2,1)}), bf16[64,2,128,64]{2,1,3,0:T(2,128)(2,1)}, u32[]{:S(2)}, u32[]{:S(2)}) %all-to-all-start.1) | async-done | bytes 2097184 | tf_op jit(solution)/shard_map/all_to_all | solution.py:68
  396.2 3.9 abs_reduce_fusion
  400.2 4.6 fusion.7
  404.7 0.7 copy.68
  405.4 40.4 %all-gather.12.cloned.1.call-done = f32[32768,64]{0,1:T(8,128)} async-done(((f32[512,64]{0,1:T(8,128)}), f32[32768,64]{0,1:T(8,128)}) %all-gather.12.cloned.1.call-update) | async-done | bytes 8388624 | tf_op jit(solution)/shard_map/all_gather | solution.py:7
  445.8 8.1 %copy.52 = f32[8,8,64,512]{3,2,1,0:T(8,128)S(1)} copy(f32[8,8,64,512]{3,1,2,0:T(8,128)} %bitcast.62) | data formatting | bytes 16777216
  453.9 2.4 bitcast_reduce_fusion
  456.3 0.7 broadcast_multiply_fusion
  (30 shorter events, 0.5 us)
Async XLA Ops:
  7.2 177.6 %copy-start = (bf16[64,128,128]{2,1,0:T(8,128)(2,1)S(1)}, bf16[64,128,128]{2,1,0:T(8,128)(2,1)}, u32[]{:S(2)}) copy-start(bf16[64,128,128]{2,1,0:T(8,128)(2,1)} %param.9) | copy-start | bytes 6291460
  7.2 164.4 %all-gather.6.cloned.1.call-start = ((), (), s32[]{:S(2)}) async-start(), calls=%async_computation.2 | async-start | bytes 8519680 | tf_op jit(solution)/shard_map/all_gather | solution.py:27
  7.9 208.2 %all-gather.8.cloned.1.call-start = ((), (), s32[]{:S(2)}) async-start(), calls=%async_computation.3 | async-start | bytes 1179648 | tf_op jit(solution)/shard_map/all_gather | solution.py:35
  184.8 1.5 copy-start.3
  186.3 29.8 %copy-start.4 = (s32[1024]{0:T(1024)S(1)}, s32[1024]{0:T(1024)}, u32[]{:S(2)}) copy-start(s32[1024]{0:T(1024)} %param.13) | copy-start | bytes 12292
  189.0 60.9 %all-gather.10.cloned.1.call-start = ((), (), s32[]{:S(2)}) async-start(), calls=%async_computation.4 | async-start | bytes 1179648 | tf_op jit(solution)/shard_map/all_gather | solution.py:46
  189.0 31.7 %copy-start.5 = (s32[64,1]{0,1:T(1,128)S(1)}, s32[64,1]{0,1:T(1,128)}, u32[]{:S(2)}) copy-start(s32[64,1]{0,1:T(1,128)} %param.11) | copy-start | bytes 772
  189.1 31.9 %copy-start.2 = (s32[64]{0:T(128)S(1)}, s32[64]{0:T(128)}, u32[]{:S(2)}) copy-start(s32[64]{0:T(128)} %param.12) | copy-start | bytes 772
  216.1 2.6 copy-start.1
  218.7 227.1 %all-gather.12.cloned.1.call-start = ((), (), s32[]{:S(2)}) async-start(), calls=%async_computation.5 | async-start | bytes 8519680 | tf_op jit(solution)/shard_map/all_gather | solution.py:7
  225.2 48.5 %all-to-all-start = ((s32[64,1,2]{2,1,0:T(1,128)}), s32[64,1,2]{2,1,0:T(1,128)S(1)}, u32[]{:S(2)}, u32[]{:S(2)}) async-start(s32[64,1,2]{2,1,0:T(1,128)} %copy.42), calls=%async_computation | async-start | bytes 65536 | tf_op jit(solution)/shard_map/all_to_all | solution.py:71
  273.7 122.5 %all-to-all-start.1 = ((bf16[64,2,128,64]{2,1,3,0:T(2,128)(2,1)}), bf16[64,2,128,64]{2,1,3,0:T(2,128)(2,1)}, u32[]{:S(2)}, u32[]{:S(2)}) async-start(bf16[64,2,128,64]{2,1,3,0:T(2,128)(2,1)} %copy.45), calls=%async_computation.1 | async-start | bytes 4194304 | tf_op jit(solution)/shard_map/all_to_all | solution.py:68
Sparse Core Ops, SparseCore 0:
  11.0 160.5 all-gather.5
  189.1 26.9 all-gather.7
  218.9 30.9 all-gather.9
  253.2 192.4 all-gather.11
